TPU v7x, 32 devices: a whole 2x2x4 slice. The times are simulated.
32 devices in a mesh: pt: 8 (over y, x, core), md: 4 (over z).
Axes of the slice: x: 2, y: 2, z: 4, core: 2. Of those that a mesh axis runs over, the one named last changes fastest.
Arguments:
- grid_index: int32 [3, 8192], P(None, 'pt'), may hold values from 0 to 255, as said below
- wavenumbers: int32 [3, 32768], P(None, 'md'), may hold values from -16 to 15, as said below
- test_block: int32 [32768, 256], P('md'), may hold values from -64 to 63
- slab_counts: int32 [8], P('pt'), may hold values from 1 to 1024, as said below
Outputs:
- adjoint_sketch: float32 [32768, 512], P(('md', 'pt'))
Inputs may be any that keep to these rules, and one draw needn't show every extreme that they name: Each slab's live points are its first slab_counts slots; in every draw one slab is full with 1024. `grid_index`: every slot's point lies in the ball of radius 256 // 2 - 1 about the grid cell (128, 128, 128). `wavenumbers`: the columns are the 32 x 32 x 32 tensor grid of wavenumber triples, each exactly once, in some order.
All inputs are finite; a program needn't handle non-finite values.
Results may differ from a plain program's by a relative error of at most 0.002.
Values may be sent and summed in bfloat16 or wider, within the bound.
A program may use at most 192 MiB of HBM per device.

v0:
```python
import math
import jax
import jax.numpy as jnp
from jax import lax
from jax.sharding import PartitionSpec as P

M = 32768
PERIOD = 512


def phase_pair(coords, wave_cols, row_start, block, live_rows):
    rows = lax.dynamic_slice_in_dim(coords, row_start, block, 1)
    turns = (
        rows[0][:, None] * wave_cols[0][None, :]
        + rows[1][:, None] * wave_cols[1][None, :]
        + rows[2][:, None] * wave_cols[2][None, :]
    )
    turns = jnp.mod(turns, PERIOD)
    angles = turns.astype(jnp.float32) * (2.0 * math.pi / PERIOD)
    in_use = row_start + jnp.arange(block, dtype=jnp.int32) < live_rows
    tile_re = jnp.where(in_use[:, None], jnp.cos(angles), 0.0).astype(jnp.bfloat16)
    tile_im = jnp.where(in_use[:, None], jnp.sin(angles), 0.0).astype(jnp.bfloat16)
    return (tile_re, tile_im)


def adjoint_piece(tile_re, tile_im, rows, width):
    dims = (((0,), (0,)), ((), ()))
    from_re = lax.dot_general(tile_re, rows, dims, preferred_element_type=jnp.float32)
    from_im = lax.dot_general(tile_im, rows, dims, preferred_element_type=jnp.float32)
    return jnp.concatenate(
        [from_re[:, :width] + from_im[:, width:], from_re[:, width:] - from_im[:, :width]], axis=1
    )


def per_device(grid_index, wavenumbers, test_block, slab_counts):
    capacity = grid_index.shape[1]
    width = test_block.shape[1]
    block = min(512, capacity)
    test_bf = test_block.astype(jnp.bfloat16)
    y_scale = 1.0 / (32.0 * math.sqrt(M))
    w_scale = 1.0 / math.sqrt(capacity * lax.axis_size("pt"))
    live_rows = slab_counts[0]
    block_count = (live_rows + block - 1) // block
    modes_local = wavenumbers.shape[1]

    def sketch_step(step_index, summed):
        row_start = step_index * block
        tile_re, tile_im = phase_pair(grid_index, wavenumbers, row_start, block, live_rows)
        part = jnp.concatenate(
            [
                jnp.dot(tile_re, test_bf, preferred_element_type=jnp.float32),
                jnp.dot(tile_im, test_bf, preferred_element_type=jnp.float32),
            ],
            axis=1,
        )
        return lax.dynamic_update_slice_in_dim(summed, part, row_start, 0)

    partial_value = lax.fori_loop(
        0, block_count, sketch_step, jnp.zeros((capacity, 2 * width), jnp.float32)
    )
    sketch = (lax.psum(partial_value, "md") * y_scale).astype(jnp.bfloat16)

    def fresh_step(step_index, summed):
        row_start = step_index * block
        tile_re, tile_im = phase_pair(grid_index, wavenumbers, row_start, block, live_rows)
        rows = lax.dynamic_slice_in_dim(sketch, row_start, block, 0)
        return summed + adjoint_piece(tile_re, tile_im, rows, width)

    summed = lax.fori_loop(
        0,
        block_count,
        fresh_step,
        jnp.zeros(
            (modes_local // lax.axis_size("pt") * lax.axis_size("pt"), 2 * width), jnp.float32
        ),
    )
    return lax.psum_scatter(summed * w_scale, "pt", scatter_dimension=0, tiled=True)


def solution(mesh):
    placed = (P(None, "pt"), P(None, "md"), P("md", None), P("pt"))
    return jax.shard_map(
        per_device, mesh=mesh, in_specs=placed, out_specs=P(("md", "pt"), None), check_vma=False
    )
```

profile of v0, /device:TPU:0, one launch (start us, length us, event | category | flops | bytes accessed | tf_op | source)
XLA Modules:
  0.0 944.1 jit_solution(14429266977389757838)
XLA Ops:
  6.5 0.0 all-reduce.2.cloned.1.call-start
  7.2 6.0 convert_element_type.42
  13.2 1.6 broadcast_in_dim.53.clone
  14.8 141.9 %while.24 = (s32[]{:T(128)}, f32[1024,512]{1,0:T(8,128)}, s32[]{:T(128)}, s32[]{:T(128)}, s32[3,1024]{1,0:T(4,128)}, /*index=5*/s32[3,8192]{1,0:T(4,128)}, bf16[...) while((s32[]{:T(128)}, f32[1024,512]{1,0:T(8,128)}, ...), condition=%wide.region_1.2_spmd, body=%wide.region_0.1_spmd.sunk | while | flops 4463002624 | bytes 66479860 | solution.py:58
  14.8 0.8 add_compare_fusion.4
  15.6 1.0 constant_dynamic-slice_fusion.4
  16.6 1.2 fusion.80
  17.8 65.0 %select_convert_fusion.25 = bf16[512,8192]{1,0:T(8,128)(2,1)S(1)} fusion(s32[8192]{0:T(1024)S(1)} %bitcast.60, s32[512]{0:T(512)S(1)} %bitcast.74, s32[8192]{0:T(1024)S(1)} %bitcast.62, s32[512]{0:T(512)S(1)} %bitcast.72, s32[8192]{0:T(1024)S(1)} %bitcast.58, s32[512]{0:T(512)S(1)} %bitcast.70, pred[512]{0:T(512)(128)(4,1)S(1)} %add_compare_fusion.4), kind=kLoop, calls=%fused_computation.7.clone.clone.1.clone.1 | loop fusion | flops 83886080 | bytes 8493568 | tf_op jit(solution)/shard_map/while/body/dot_general | solution.py:51
  82.8 4.6 fusion.82
  87.4 65.5 %select_convert_fusion.24 = bf16[512,8192]{1,0:T(8,128)(2,1)S(1)} fusion(s32[8192]{0:T(1024)S(1)} %bitcast.61, s32[512]{0:T(512)S(1)} %bitcast.75, s32[8192]{0:T(1024)S(1)} %bitcast.63, s32[512]{0:T(512)S(1)} %bitcast.73, s32[8192]{0:T(1024)S(1)} %bitcast.59, s32[512]{0:T(512)S(1)} %bitcast.71, pred[512]{0:T(512)(128)(4,1)S(1)} %add_compare_fusion.4), kind=kLoop, calls=%fused_computation.6.clone.clone.1.clone.1 | loop fusion | flops 83886080 | bytes 8493568 | tf_op jit(solution)/shard_map/while/body/dot_general | solution.py:52
  152.9 0.0 copy-done.1
  152.9 2.4 fusion.81
  155.2 0.1 pad_maximum_fusion.2
  155.3 0.3 copy.10
  155.7 1.0 constant_dynamic-update-slice_fusion.2
  156.7 0.0 all-reduce.2.cloned.1.call-update
  156.7 0.0 reduce-scatter.2.cloned.1.call-start
  156.8 230.3 %all-reduce.2.cloned.1.call-done = f32[1024,512]{1,0:T(8,128)} async-done(((f32[1024,512]{1,0:T(8,128)}), f32[1024,512]{1,0:T(8,128)}) %all-reduce.2.cloned.1.call-update) | async-done | bytes 2097168 | tf_op jit(solution)/shard_map/psum | solution.py:61
  387.1 1.9 multiply_convert_fusion
  388.9 7.8 broadcast_in_dim.52
  396.7 199.6 %while.25 = (s32[]{:T(128)}, f32[8192,512]{0,1:T(8,128)}, s32[]{:T(128)}, s32[]{:T(128)}, s32[3,1024]{1,0:T(4,128)}, /*index=5*/s32[3,8192]{1,0:T(4,128)S(1)}, b...) while((s32[]{:T(128)}, f32[8192,512]{0,1:T(8,128)}, ...), condition=%wide.region_4.5_spmd, body=%wide.region_3.4_spmd.sunk | while | flops 8770290688 | bytes 137783024 | solution.py:69
  408.6 0.7 add_compare_fusion.5
  409.3 0.9 constant_dynamic-slice_fusion.5
  410.2 0.1 fusion.85
  410.4 67.4 %fusion.89 = f32[8192,512]{0,1:T(8,128)} fusion(s32[8192]{0:T(1024)S(1)} %bitcast.66, s32[512]{0:T(512)S(1)} %bitcast.80, s32[8192]{0:T(1024)S(1)} %bitcast.68, s32[512]{0:T(512)S(1)} %bitcast.78, s32[8192]{0:T(1024)S(1)} %bitcast.64, s32[512]{0:T(512)S(1)} %bitcast.76, pred[512]{0:T(512)(128)(4,1)S(1)} %add_compare_fusion.5, ...), kind=kOutput, calls=%fused_computation.37.clone.3 | convolution fusion | flops 4378853376 | bytes 17406464 | tf_op jit(solution)/shard_map/while/body/dot_general | solution.py:28
  477.7 81.0 %fusion.87 = f32[8192,512]{0,1:T(8,128)} fusion(s32[8192]{0:T(1024)S(1)} %bitcast.67, s32[512]{0:T(512)S(1)} %bitcast.81, s32[8192]{0:T(1024)S(1)} %bitcast.69, s32[512]{0:T(512)S(1)} %bitcast.79, s32[8192]{0:T(1024)S(1)} %bitcast.65, s32[512]{0:T(512)S(1)} %bitcast.77, pred[512]{0:T(512)(128)(4,1)S(1)} %add_compare_fusion.5, ...), kind=kOutput, calls=%fused_computation.38.clone.3 | convolution fusion | flops 4378853376 | bytes 17406464 | tf_op jit(solution)/shard_map/while/body/dot_general | solution.py:29
  558.7 18.0 %slice_add_fusion.2 = (f32[8192,256]{0,1:T(8,128)}, f32[8192,256]{0,1:T(8,128)}) fusion(f32[8192,512]{0,1:T(8,128)} %fusion.87, f32[8192,512]{0,1:T(8,128)} %fusion.89), kind=kLoop, calls=%fused_computation.40.clone.1 | loop fusion | flops 4194304 | bytes 50331648 | tf_op jit(solution)/shard_map/while/body/add | solution.py:31
  576.8 17.2 %maximum_add_fusion.2 = f32[8192,512]{0,1:T(8,128)} fusion(f32[8192,512]{0,1:T(8,128)} %get-tuple-element.404, f32[8192,256]{0,1:T(8,128)} %get-tuple-element.349, f32[8192,256]{0,1:T(8,128)} %get-tuple-element.350), kind=kLoop, calls=%fused_computation.34.clone.1 | loop fusion | flops 8388608 | bytes 50331648 | tf_op jit(solution)/shard_map/while/body/add | solution.py:67
  596.3 17.4 %copy.6 = f32[8192,512]{1,0:T(8,128)} copy(f32[8192,512]{0,1:T(8,128)} %get-tuple-element.192) | data formatting | bytes 33554432 | tf_op jit(solution)/shard_map/while | solution.py:69
  613.8 11.7 %broadcast_multiply_fusion = f32[8192,512]{1,0:T(8,128)} fusion(f32[8192,512]{1,0:T(8,128)} %copy.6), kind=kLoop, calls=%fused_computation.59 | loop fusion | flops 4194304 | bytes 33554432 | tf_op jit(solution)/shard_map/mul | solution.py:77
  625.5 0.0 reduce-scatter.2.cloned.1.call-update
  625.5 311.4 %reduce-scatter.2.cloned.1.call-done = f32[1024,512]{1,0:T(8,128)} async-done(((f32[8192,512]{1,0:T(8,128)}), f32[1024,512]{1,0:T(8,128)}) %reduce-scatter.2.cloned.1.call-update) | async-done | bytes 2097168 | tf_op jit(solution)/shard_map/reduce_scatter | solution.py:77
  (5 shorter events, 0.1 us)
Async XLA Ops:
  6.5 380.5 %all-reduce.2.cloned.1.call-start = ((), (), s32[]{:S(2)}) async-start(), calls=%async_computation.1 | async-start | bytes 4194304 | tf_op jit(solution)/shard_map/psum | solution.py:61
  14.8 138.1 %copy-start.1 = (bf16[8192,256]{1,0:T(8,128)(2,1)S(1)}, bf16[8192,256]{1,0:T(8,128)(2,1)}, u32[]{:S(2)}) copy-start(bf16[8192,256]{1,0:T(8,128)(2,1)} %get-tuple-element.383) | copy-start | bytes 12582916 | tf_op jit(solution)/shard_map/while
  156.7 240.0 %copy-start = (s32[3,8192]{1,0:T(4,128)S(1)}, s32[3,8192]{1,0:T(4,128)}, u32[]{:S(2)}) copy-start(s32[3,8192]{1,0:T(4,128)} %get-tuple-element.435) | copy-start | bytes 294916
  156.7 780.2 %reduce-scatter.2.cloned.1.call-start = ((), (), s32[]{:S(2)}) async-start(), calls=%async_computation.2 | async-start | bytes 18874368 | tf_op jit(solution)/shard_map/reduce_scatter | solution.py:77
Sparse Core Ops, SparseCore 0:
  156.8 230.1 all-reduce.1
  625.7 311.2 reduce-scatter.1
where the time goes:
time: 945 us; the launch traced here: 944 us
  waiting for transfers between devices  542 us (57%)
  other arithmetic  187 us (20%)
  matrix products  155 us (16%)
  local copies, waits for them, and re-layouts  31.4 us (3%)
  loops' own time  14.4 us (2%)
  between operations  14.4 us (2%)
    reduce_scatter x1, waiting for transfers between devices, per_device(): lax.psum_scatter(summed * w_scale, 'pt', scatter_dimension=0, tiled=True)  311 us
    psum x1, waiting for transfers between devices, per_device(): sketch = (lax.psum(partial_value, 'md') * y_scale).astype(jnp.bfloat16)  230 us
    dot_general x1, matrix products, adjoint_piece(): lax.dot_general(tile_im, rows, dims, preferred_element_type=jnp.float32)  81 us
    dot_general x1, matrix products, adjoint_piece(): lax.dot_general(tile_re, rows, dims, preferred_element_type=jnp.float32)  67.4 us
    dot_general x1, other arithmetic, sketch_step(): jnp.dot(tile_im, test_bf, preferred_element_type=jnp.float32)  65.5 us
    dot_general x1, other arithmetic, sketch_step(): jnp.dot(tile_re, test_bf, preferred_element_type=jnp.float32)  65 us
  transfers between devices with their start and end apart: 2, of which 2 were waited for; matrix products, arithmetic and copies ran while one was open for 0% of the time, Pallas kernels for 0%

commit v1 on v0

--- a/solution.py
+++ b/solution.py
@@ -58,7 +58,11 @@
     partial_value = lax.fori_loop(
         0, block_count, sketch_step, jnp.zeros((capacity, 2 * width), jnp.float32)
     )
-    sketch = (lax.psum(partial_value, "md") * y_scale).astype(jnp.bfloat16)
+
+    def scan_counts(point):
+        return jax.lax.all_gather(point, "md").sum(axis=0)
+
+    sketch = (scan_counts(partial_value) * y_scale).astype(jnp.bfloat16)
 
     def fresh_step(step_index, summed):
         row_start = step_index * block

time: 945 us -> 1010 us (1.069); the launches traced: 944 us -> 992 us
  waiting for transfers between devices: 542 us -> 577 us
  matrix products: 155 us -> 141 us
  loops' own time: 14.4 us -> 25.7 us
    all_gather x0 -> x1, waiting for transfers between devices: none -> 292 us  [scan_counts(): return jax.lax.all_gather(point, 'md').sum(axis=0)]
    psum x1 -> x0, waiting for transfers between devices: 230 us -> none  [per_device(): sketch = (lax.psum(partial_value, 'md') * y_scale).astype(jnp.bfloat16)]
    reduce_scatter x1, waiting for transfers between devices: 311 us -> 284 us  [per_device(): lax.psum_scatter(summed * w_scale, 'pt', scatter_dimension=0, tiled=True)]
    dot_general x1, matrix products: 81 us -> 67.2 us  [adjoint_piece(): lax.dot_general(tile_im, rows, dims, preferred_element_type=jnp.float32)]
    another operation x1, loops' own time: 14.3 us -> 25.2 us  [per_device(): lax.fori_loop(0, block_count, fresh_step, jnp.zeros((modes_local // lax.a...]
    all_gather x0 -> x1, local copies, waits for them, and re-layouts: none -> 10.8 us  [scan_counts(): return jax.lax.all_gather(point, 'md').sum(axis=0)]
where the time goes in v1:
time: 1010 us; the launch traced here: 992 us
  waiting for transfers between devices  577 us (57%)
  other arithmetic  194 us (19%)
  matrix products  141 us (14%)
  local copies, waits for them, and re-layouts  40.8 us (4%)
  loops' own time  25.7 us (3%)
  between operations  14.3 us (1%)
    all_gather x1, waiting for transfers between devices, scan_counts(): return jax.lax.all_gather(point, 'md').sum(axis=0)  292 us
    reduce_scatter x1, waiting for transfers between devices, per_device(): lax.psum_scatter(summed * w_scale, 'pt', scatter_dimension=0, tiled=True)  284 us
    dot_general x1, matrix products, adjoint_piece(): lax.dot_general(tile_im, rows, dims, preferred_element_type=jnp.float32)  67.2 us
    dot_general x1, matrix products, adjoint_piece(): lax.dot_general(tile_re, rows, dims, preferred_element_type=jnp.float32)  66.8 us
    dot_general x1, other arithmetic, sketch_step(): jnp.dot(tile_im, test_bf, preferred_element_type=jnp.float32)  65.5 us
    dot_general x1, other arithmetic, sketch_step(): jnp.dot(tile_re, test_bf, preferred_element_type=jnp.float32)  65 us
    another operation x1, loops' own time, per_device(): lax.fori_loop(0, block_count, fresh_step, jnp.zeros((modes_local // lax.a...  25.2 us
  transfers between devices with their start and end apart: 2, of which 2 were waited for; matrix products, arithmetic and copies ran while one was open for 0% of the time, Pallas kernels for 0%

profile of v1, /device:TPU:0, one launch (start us, length us, event | category | flops | bytes accessed | tf_op | source)
XLA Modules:
  0.0 992.1 jit_solution(1939257350669611383)
XLA Ops:
  7.2 6.0 convert_element_type.42
  13.2 0.2 broadcast_in_dim.53
  13.5 141.0 %while.24 = (s32[]{:T(128)}, f32[1024,512]{0,1:T(8,128)S(1)}, s32[]{:T(128)}, s32[]{:T(128)}, s32[3,1024]{1,0:T(4,128)}, /*index=5*/s32[3,8192]{1,0:T(4,128)}, b...) while((s32[]{:T(128)}, f32[1024,512]{0,1:T(8,128)S(1)}, ...), condition=%wide.region_1.2_spmd, body=%wide.region_0.1_spmd.sunk | while | flops 4463002624 | bytes 62285556 | solution.py:58
  13.5 0.8 add_compare_fusion.4
  14.3 1.0 constant_dynamic-slice_fusion.4
  15.3 1.2 fusion.80
  16.5 65.0 %select_convert_fusion.25 = bf16[512,8192]{1,0:T(8,128)(2,1)S(1)} fusion(s32[8192]{0:T(1024)S(1)} %bitcast.62, s32[512]{0:T(512)S(1)} %bitcast.76, s32[8192]{0:T(1024)S(1)} %bitcast.64, s32[512]{0:T(512)S(1)} %bitcast.74, s32[8192]{0:T(1024)S(1)} %bitcast.60, s32[512]{0:T(512)S(1)} %bitcast.72, pred[512]{0:T(512)(128)(4,1)S(1)} %add_compare_fusion.4), kind=kLoop, calls=%fused_computation.7.clone.clone.1.clone.1 | loop fusion | flops 83886080 | bytes 8493568 | tf_op jit(solution)/shard_map/while/body/dot_general | solution.py:51
  81.5 4.6 fusion.82
  86.1 65.5 %select_convert_fusion.24 = bf16[512,8192]{1,0:T(8,128)(2,1)S(1)} fusion(s32[8192]{0:T(1024)S(1)} %bitcast.63, s32[512]{0:T(512)S(1)} %bitcast.77, s32[8192]{0:T(1024)S(1)} %bitcast.65, s32[512]{0:T(512)S(1)} %bitcast.75, s32[8192]{0:T(1024)S(1)} %bitcast.61, s32[512]{0:T(512)S(1)} %bitcast.73, pred[512]{0:T(512)(128)(4,1)S(1)} %add_compare_fusion.4), kind=kLoop, calls=%fused_computation.6.clone.clone.1.clone.1 | loop fusion | flops 83886080 | bytes 8493568 | tf_op jit(solution)/shard_map/while/body/dot_general | solution.py:52
  151.6 2.4 fusion.81
  153.9 0.1 maximum_dynamic-update-slice_fusion.2
  154.4 0.0 copy-start
  154.4 1.3 copy-done
  155.8 0.0 all-gather.3.cloned.1.call-update
  155.8 0.0 reduce-scatter.2.cloned.1.call-start
  155.8 292.1 %all-gather.3.cloned.1.call-done = f32[4096,512]{0,1:T(8,128)} async-done(((f32[1024,512]{0,1:T(8,128)}), f32[4096,512]{0,1:T(8,128)}) %all-gather.3.cloned.1.call-update) | async-done | bytes 8388624 | tf_op jit(solution)/shard_map/all_gather | solution.py:63
  447.9 10.8 %reshape.16 = f32[4,1024,512]{1,0,2:T(4,128)} reshape(f32[4096,512]{0,1:T(8,128)} %all-gather.3.cloned.1.call-done) | data formatting | bytes 16777216 | tf_op jit(solution)/shard_map/all_gather | solution.py:63
  458.7 8.5 reduce_sum.9
  467.2 0.3 multiply_convert_fusion
  467.5 7.8 broadcast_in_dim.52
  475.2 196.2 %while.25 = (s32[]{:T(128)}, f32[8192,512]{0,1:T(8,128)}, s32[]{:T(128)}, s32[]{:T(128)}, s32[3,1024]{1,0:T(4,128)}, /*index=5*/s32[3,8192]{1,0:T(4,128)S(1)}, b...) while((s32[]{:T(128)}, f32[8192,512]{0,1:T(8,128)}, ...), condition=%wide.region_4.5_spmd, body=%wide.region_3.4_spmd.sunk | while | flops 8770290688 | bytes 137783024 | solution.py:73
  498.8 0.7 add_compare_fusion.5
  499.5 0.9 constant_dynamic-slice_fusion.5
  500.4 0.1 fusion.85
  500.6 66.8 %fusion.89 = f32[8192,512]{0,1:T(8,128)} fusion(s32[8192]{0:T(1024)S(1)} %bitcast.68, s32[512]{0:T(512)S(1)} %bitcast.82, s32[8192]{0:T(1024)S(1)} %bitcast.70, s32[512]{0:T(512)S(1)} %bitcast.80, s32[8192]{0:T(1024)S(1)} %bitcast.66, s32[512]{0:T(512)S(1)} %bitcast.78, pred[512]{0:T(512)(128)(4,1)S(1)} %add_compare_fusion.5, ...), kind=kOutput, calls=%fused_computation.36.clone.3 | convolution fusion | flops 4378853376 | bytes 17406464 | tf_op jit(solution)/shard_map/while/body/dot_general | solution.py:28
  567.4 67.2 %fusion.87 = f32[8192,512]{0,1:T(8,128)} fusion(s32[8192]{0:T(1024)S(1)} %bitcast.69, s32[512]{0:T(512)S(1)} %bitcast.83, s32[8192]{0:T(1024)S(1)} %bitcast.71, s32[512]{0:T(512)S(1)} %bitcast.81, s32[8192]{0:T(1024)S(1)} %bitcast.67, s32[512]{0:T(512)S(1)} %bitcast.79, pred[512]{0:T(512)(128)(4,1)S(1)} %add_compare_fusion.5, ...), kind=kOutput, calls=%fused_computation.37.clone.3 | convolution fusion | flops 4378853376 | bytes 17406464 | tf_op jit(solution)/shard_map/while/body/dot_general | solution.py:29
  634.6 18.0 %slice_add_fusion.2 = (f32[8192,256]{0,1:T(8,128)}, f32[8192,256]{0,1:T(8,128)}) fusion(f32[8192,512]{0,1:T(8,128)} %fusion.87, f32[8192,512]{0,1:T(8,128)} %fusion.89), kind=kLoop, calls=%fused_computation.39.clone.1 | loop fusion | flops 4194304 | bytes 50331648 | tf_op jit(solution)/shard_map/while/body/add | solution.py:31
  652.6 17.3 %maximum_add_fusion.2 = f32[8192,512]{0,1:T(8,128)} fusion(f32[8192,512]{0,1:T(8,128)} %get-tuple-element.411, f32[8192,256]{0,1:T(8,128)} %get-tuple-element.356, f32[8192,256]{0,1:T(8,128)} %get-tuple-element.357), kind=kLoop, calls=%fused_computation.33.clone.1 | loop fusion | flops 8388608 | bytes 50331648 | tf_op jit(solution)/shard_map/while/body/add | solution.py:71
  671.4 17.4 %copy.7 = f32[8192,512]{1,0:T(8,128)} copy(f32[8192,512]{0,1:T(8,128)} %get-tuple-element.192) | data formatting | bytes 33554432 | tf_op jit(solution)/shard_map/while | solution.py:73
  688.9 11.7 %broadcast_multiply_fusion = f32[8192,512]{1,0:T(8,128)} fusion(f32[8192,512]{1,0:T(8,128)} %copy.7), kind=kLoop, calls=%fused_computation.58 | loop fusion | flops 4194304 | bytes 33554432 | tf_op jit(solution)/shard_map/mul | solution.py:81
  700.6 0.0 reduce-scatter.2.cloned.1.call-update
  700.6 284.5 %reduce-scatter.2.cloned.1.call-done = f32[1024,512]{1,0:T(8,128)} async-done(((f32[8192,512]{1,0:T(8,128)}), f32[1024,512]{1,0:T(8,128)}) %reduce-scatter.2.cloned.1.call-update) | async-done | bytes 2097168 | tf_op jit(solution)/shard_map/reduce_scatter | solution.py:81
  (7 shorter events, 0.1 us)
Async XLA Ops:
  6.5 441.4 %all-gather.3.cloned.1.call-start = ((), (), s32[]{:S(2)}) async-start(), calls=%async_computation.2 | async-start | bytes 10485760 | tf_op jit(solution)/shard_map/all_gather | solution.py:63
  13.5 138.1 %copy-start.2 = (bf16[8192,256]{1,0:T(8,128)(2,1)S(1)}, bf16[8192,256]{1,0:T(8,128)(2,1)}, u32[]{:S(2)}) copy-start(bf16[8192,256]{1,0:T(8,128)(2,1)} %get-tuple-element.390) | copy-start | bytes 12582916 | tf_op jit(solution)/shard_map/while
  154.4 1.3 copy-start
  155.8 829.3 %reduce-scatter.2.cloned.1.call-start = ((), (), s32[]{:S(2)}) async-start(), calls=%async_computation.1 | async-start | bytes 18874368 | tf_op jit(solution)/shard_map/reduce_scatter | solution.py:81
  458.7 16.5 %copy-start.1 = (s32[3,8192]{1,0:T(4,128)S(1)}, s32[3,8192]{1,0:T(4,128)}, u32[]{:S(2)}) copy-start(s32[3,8192]{1,0:T(4,128)} %get-tuple-element.443) | copy-start | bytes 294916
Sparse Core Ops, SparseCore 0:
  155.9 291.9 all-gather.2
  700.8 284.2 reduce-scatter.1
